TPU v7x, 256 devices: a whole 4x4x8 slice. The times are simulated.
256 devices in a mesh: imp: 32 (over z, y_hi, core), cre: 8 (over x, y_lo).
Axes of the slice: x: 4, y: 4 (y_hi: 2, y_lo: 2; y = y_hi * 2 + y_lo), z: 8, core: 2. Of those that a mesh axis runs over, the one named last changes fastest.
Arguments:
- impressions: bfloat16 [32768, 256], P('imp'), may hold values from -24 to 24
- panels: bfloat16 [8, 2048, 256], P('cre', 'imp'), may hold values from -2 to 2
- block_lists: int32 [256, 16], P('imp'), may hold values from 0 to 127, as said below
- block_counts: int32 [256], P('imp'), may hold values from 1 to 16, as said below
- imp_weight: float32 [32768], P('imp'), may hold values from 0.2 to 5
- spend_goals: float32 [8, 2048], P('cre', 'imp'), may hold values from 0.2 to 5
- prices: float32 [8, 2048], P('cre', 'imp'), may hold values from -1 to 1
Outputs:
- final_prices: float32 [8, 2048], P('cre', 'imp')
- final_spend: float32 [8, 2048], P('cre', 'imp')
- log_norm: float32 [32768], P('imp')
Inputs may be any that keep to these rules, and one draw needn't show every extreme that they name: `block_lists`: each row lists 16 different block ids; only the first block_counts entries of a row are eligible for the 128 impressions of that tile, the others must be ignored. `block_counts`: some tile has 16 eligible blocks.
All inputs are finite; a program needn't handle non-finite values.
Results may differ from a plain program's by a relative error of at most 0.0003.
Values may be sent and summed in bfloat16 or wider, within the bound.
A program may use at most 64 MiB of HBM per device.

v0:
```python
import jax
import jax.numpy as jnp
from jax import lax
from jax.sharding import PartitionSpec as P

CRE_LOC = 2048
TILE = 128
BLOCK = 128
ITERS = 2
NEG_FILL = -1e30
TAU_INV = 4.0
STEP_RATE = 0.5


def block_table(block_lists, block_counts, local_blocks, cre_index):
    block_ids = cre_index * local_blocks + lax.iota(jnp.int32, local_blocks)
    in_list = lax.iota(jnp.int32, block_lists.shape[1])[None, :] < block_counts[:, None]
    matches = (block_lists[:, :, None] == block_ids[None, None, :]) & in_list[:, :, None]
    allowed = jnp.any(matches, axis=1)
    allowed = jnp.repeat(allowed, TILE, axis=0)
    return jnp.repeat(allowed, BLOCK, axis=1)


def scored(impressions, panel_rows, price_rows, col_mask):
    affinity = lax.dot_general(
        impressions, panel_rows, (((1,), (1,)), ((), ())), preferred_element_type=jnp.float32
    )
    logit_vals = TAU_INV * affinity + price_rows[None, :]
    return jnp.where(col_mask, logit_vals, NEG_FILL)


def sweep(panel_rows, group_prices, mask_full, running, update):
    col_count = panel_rows.shape[0]
    sub_width = 512

    def inner(current, step_index):
        shift_cols = step_index * sub_width
        part_panel = lax.dynamic_slice_in_dim(panel_rows, shift_cols, sub_width, 0)
        part_price = lax.dynamic_slice_in_dim(group_prices, shift_cols, sub_width, 0)
        part_mask = lax.dynamic_slice_in_dim(mask_full, shift_cols, sub_width, 1)
        return (update(current, part_panel, part_price, part_mask, shift_cols), None)

    current, _ = lax.scan(inner, running, jnp.arange(col_count // sub_width, dtype=jnp.int32))
    return current


def shards(impressions, panels, block_lists, block_counts, imp_weight, spend_goals, prices):
    local_blocks = CRE_LOC // BLOCK
    mask_full = block_table(block_lists, block_counts, local_blocks, lax.axis_index("cre"))
    imp_rows = impressions.shape[0]
    owned_rows = prices.shape[1]
    owned_start = lax.axis_index("imp") * owned_rows

    def max_step(current, panel_rows, price_rows, col_mask, first_col):
        row_top, row_total = current
        masked = scored(impressions, panel_rows, price_rows, col_mask)
        block_top = jnp.max(masked, axis=1)
        new_top = jnp.maximum(row_top, block_top)
        block_sum = jnp.sum(jnp.where(col_mask, jnp.exp(masked - block_top[:, None]), 0.0), axis=1)
        return (
            new_top,
            row_total * jnp.exp(row_top - new_top) + block_sum * jnp.exp(block_top - new_top),
        )

    spend_owned = None
    row_norm = None
    for iteration in range(ITERS):
        start_state = (
            jnp.full((imp_rows,), NEG_FILL, jnp.float32),
            jnp.zeros((imp_rows,), jnp.float32),
        )
        empty_spend = jnp.zeros((CRE_LOC,), jnp.float32)
        whole_prices = lax.all_gather(prices, "imp", axis=1, tiled=True)[0]
        row_top, row_total = sweep(
            lax.all_gather(panels, "imp", axis=1, tiled=True)[0],
            whole_prices,
            mask_full,
            start_state,
            max_step,
        )
        merged_top = lax.pmax(row_top, "cre")
        row_total = lax.psum(row_total * jnp.exp(row_top - merged_top), "cre")
        row_top = merged_top
        row_norm = row_top + jnp.log(row_total)

        def spend_step(current, panel_rows, price_rows, col_mask, first_col):
            masked = scored(impressions, panel_rows, price_rows, col_mask)
            shares = jnp.where(col_mask, jnp.exp(masked - row_norm[:, None]), 0.0)
            col_spend = jnp.sum(imp_weight[:, None] * shares, axis=0)
            return lax.dynamic_update_slice_in_dim(current, col_spend, first_col, 0)

        partial_spend = sweep(
            lax.all_gather(panels, "imp", axis=1, tiled=True)[0],
            whole_prices,
            mask_full,
            empty_spend,
            spend_step,
        )
        summed = lax.psum(partial_spend, "imp")
        spend_owned = lax.dynamic_slice_in_dim(summed, owned_start, owned_rows, 0)
        spend_owned = spend_owned.reshape(1, owned_rows)
        prices = prices + STEP_RATE * (
            jnp.log(spend_goals) - jnp.log(spend_owned + 0.25 * spend_goals)
        )
    return (prices, spend_owned, row_norm)


def solution(mesh):
    placed = (
        P("imp", None),
        P("cre", "imp", None),
        P("imp", None),
        P("imp"),
        P("imp"),
        P("cre", "imp"),
        P("cre", "imp"),
    )
    return jax.shard_map(
        shards,
        mesh=mesh,
        in_specs=placed,
        out_specs=(P("cre", "imp"), P("cre", "imp"), P("imp")),
        check_vma=False,
    )
```

profile of v0, /device:TPU:1, one launch (start us, length us, event | category | flops | bytes accessed | tf_op | source)
XLA Modules:
  0.0 427.9 jit_solution(15510092804575440473)
XLA Ops:
  7.2 0.7 all-gather.2.cloned.1.call-update
  8.0 0.7 iota_compare_fusion
  8.7 0.8 and_reduce_fusion
  9.7 1.3 dynamic-slice
  11.6 0.8 bitcast_dynamic-update-slice_fusion.1
  12.4 70.3 %all-reduce = f32[2048]{0:T(1024)S(1)} all-reduce(f32[2048]{0:T(1024)S(1)} %bitcast_dynamic-update-slice_fusion.1), channel_id=1, replica_groups=mesh['imp'=32,'cre'=8] {'imp'}, use_global_device_ids=true, to_apply=%add | all-reduce | flops 2048 | bytes 16384 | tf_op jit(solution)/shard_map/squeeze | solution.py:73
  82.8 9.8 %all-gather.2.cloned.1.call-done = bf16[1,2048,256]{2,1,0:T(8,128)(2,1)} async-done(((bf16[1,64,256]{2,1,0:T(8,128)(2,1)}), bf16[1,2048,256]{2,1,0:T(8,128)(2,1)}) %all-gather.2.cloned.1.call-update) | async-done | bytes 1048592 | tf_op jit(solution)/shard_map/all_gather | solution.py:93
  93.1 0.7 copy-done.3
  93.7 15.7 %while.48 = (s32[]{:T(128)}, f32[1024]{0:T(1024)S(1)}, f32[1024]{0:T(1024)S(1)}, s32[4]{0:T(128)S(1)}, pred[1024,2048]{0,1:T(32,128)(4,1)S(1)}, /*index=5*/bf16[...) while((s32[]{:T(128)}, f32[1024]{0:T(1024)S(1)}, ...), condition=%wide.region_4.5_spmd.clone, body=%wide.region_1.4_spmd.clone.sunk | while | flops 273684480 | bytes 6075585 | solution.py:43
  93.8 0.7 dynamic_slice.118
  95.2 1.7 fusion.49
  96.9 0.8 select_reduce_fusion.4
  97.7 0.7 dynamic_slice.118
  99.1 1.7 fusion.49
  100.8 0.8 select_reduce_fusion.4
  101.6 0.7 dynamic_slice.118
  103.0 1.7 fusion.49
  104.7 0.8 select_reduce_fusion.4
  105.5 0.7 dynamic_slice.118
  107.0 1.7 fusion.49
  108.6 0.8 select_reduce_fusion.4
  109.4 14.9 %pmax.14 = f32[1024]{0:T(1024)S(1)} all-reduce(f32[1024]{0:T(1024)S(1)} %get-tuple-element.183), channel_id=1, replica_groups=mesh['imp'=32,'cre'=8] {'cre'}, use_global_device_ids=true, to_apply=%region_5.6 | all-reduce | flops 1024 | bytes 8192 | tf_op jit(solution)/shard_map/pmax | solution.py:81
  124.4 12.5 %psum.28 = f32[1024]{0:T(1024)S(1)} all-reduce(f32[1024]{0:T(1024)S(1)} %exponential_multiply_fusion.1), channel_id=1, replica_groups=mesh['imp'=32,'cre'=8] {'cre'}, use_global_device_ids=true, to_apply=%region_6.7 | all-reduce | flops 1024 | bytes 8192 | tf_op jit(solution)/shard_map/psum | solution.py:82
  136.9 14.6 %while.46 = (s32[]{:T(128)}, f32[2048]{0:T(1024)S(1)}, f32[1024]{0:T(1024)S(1)}, s32[4]{0:T(128)S(1)}, pred[1024,2048]{0,1:T(32,128)(4,1)S(1)}, /*index=5*/bf16[...) while((s32[]{:T(128)}, f32[2048]{0:T(1024)S(1)}, ...), condition=%wide.region_9.10_spmd, body=%wide.region_7.9_spmd.sunk | while | flops 272104960 | bytes 1332415 | solution.py:43
  138.2 2.1 fusion.44
  141.9 2.1 fusion.44
  145.6 2.1 fusion.44
  149.2 2.1 fusion.44
  151.5 72.9 %psum.29 = f32[2048]{0:T(1024)S(1)} all-reduce(f32[2048]{0:T(1024)S(1)} %get-tuple-element.185), channel_id=1, replica_groups=mesh['imp'=32,'cre'=8] {'imp'}, use_global_device_ids=true, to_apply=%region_10.11 | all-reduce | flops 2048 | bytes 16384 | tf_op jit(solution)/shard_map/psum | solution.py:99
  224.6 66.0 %all-reduce.1 = f32[2048]{0:T(1024)S(1)} all-reduce(f32[2048]{0:T(1024)S(1)} %get-tuple-element.317), channel_id=1, replica_groups=mesh['imp'=32,'cre'=8] {'imp'}, use_global_device_ids=true, to_apply=%add.1 | all-reduce | flops 2048 | bytes 16384 | tf_op jit(solution)/shard_map/squeeze | solution.py:73
  290.7 15.2 %while.49 = (s32[]{:T(128)}, f32[1024]{0:T(1024)S(1)}, f32[1024]{0:T(1024)S(1)}, s32[4]{0:T(128)S(1)}, pred[1024,2048]{0,1:T(32,128)(4,1)S(1)}, /*index=5*/bf16[...) while((s32[]{:T(128)}, f32[1024]{0:T(1024)S(1)}, ...), condition=%wide.region_14.15_spmd.clone, body=%wide.region_11.14_spmd.clone.sunk | while | flops 273684480 | bytes 6075585 | solution.py:43
  292.0 1.7 fusion.52
  293.7 0.8 select_reduce_fusion.5
  295.8 1.7 fusion.52
  297.5 0.8 select_reduce_fusion.5
  299.6 1.7 fusion.52
  301.3 0.8 select_reduce_fusion.5
  303.4 1.7 fusion.52
  305.1 0.8 select_reduce_fusion.5
  305.9 14.2 %pmax.15 = f32[1024]{0:T(1024)S(1)} all-reduce(f32[1024]{0:T(1024)S(1)} %get-tuple-element.186), channel_id=1, replica_groups=mesh['imp'=32,'cre'=8] {'cre'}, use_global_device_ids=true, to_apply=%region_15.16 | all-reduce | flops 1024 | bytes 8192 | tf_op jit(solution)/shard_map/pmax | solution.py:81
  320.0 12.8 %psum.30 = f32[1024]{0:T(1024)S(1)} all-reduce(f32[1024]{0:T(1024)S(1)} %exponential_multiply_fusion), channel_id=1, replica_groups=mesh['imp'=32,'cre'=8] {'cre'}, use_global_device_ids=true, to_apply=%region_16.17 | all-reduce | flops 1024 | bytes 8192 | tf_op jit(solution)/shard_map/psum | solution.py:82
  332.8 14.6 %while.47 = (s32[]{:T(128)}, f32[2048]{0:T(1024)S(1)}, f32[1024]{0:T(1024)S(1)}, s32[4]{0:T(128)S(1)}, pred[1024,2048]{0,1:T(32,128)(4,1)S(1)}, /*index=5*/bf16[...) while((s32[]{:T(128)}, f32[2048]{0:T(1024)S(1)}, ...), condition=%wide.region_19.20_spmd, body=%wide.region_17.19_spmd.sunk | while | flops 272104960 | bytes 1332415 | solution.py:43
  334.1 2.1 fusion.47
  337.8 2.1 fusion.47
  341.5 2.1 fusion.47
  345.1 2.1 fusion.47
  347.4 73.0 %psum.31 = f32[2048]{0:T(1024)S(1)} all-reduce(f32[2048]{0:T(1024)S(1)} %get-tuple-element.188), channel_id=1, replica_groups=mesh['imp'=32,'cre'=8] {'imp'}, use_global_device_ids=true, to_apply=%region_20.21 | all-reduce | flops 2048 | bytes 16384 | tf_op jit(solution)/shard_map/psum | solution.py:99
  420.5 0.6 multiply_add_fusion
  (76 shorter events, 11.5 us)
Async XLA Ops:
  7.2 85.4 %all-gather.2.cloned.1.call-start = ((), (), s32[]{:S(2)}) async-start(), calls=%async_computation | async-start | bytes 1081344 | tf_op jit(solution)/shard_map/all_gather | solution.py:93
  92.5 1.2 copy-start.3
  93.7 43.1 %copy-start.4 = (f32[1024]{0:T(1024)S(1)}, f32[1024]{0:T(1024)}, u32[]{:S(2)}) copy-start(f32[1024]{0:T(1024)} %param.19) | copy-start | bytes 12292
  136.9 87.5 %copy-start.1 = (f32[1,64]{1,0:T(1,128)S(1)}, f32[1,64]{1,0:T(1,128)}, u32[]{:S(2)}) copy-start(f32[1,64]{1,0:T(1,128)} %param.20) | copy-start | bytes 772
  136.9 87.5 %copy-start.2 = (f32[1,64]{1,0:T(1,128)S(1)}, f32[1,64]{1,0:T(1,128)}, u32[]{:S(2)}) copy-start(f32[1,64]{1,0:T(1,128)} %param.21) | copy-start | bytes 772
  347.4 73.7 %copy-start = (f32[1024]{0:T(1024)}, f32[1024]{0:T(1024)S(1)}, u32[]{:S(2)}) copy-start(f32[1024]{0:T(1024)S(1)} %get-tuple-element.705) | copy-start | bytes 12292
Sparse Core Ops, SparseCore 0:
  10.8 81.6 all-gather.1
where the time goes:
time: 429 us; the launch traced here: 428 us
  blocking collectives  337 us (79%)
  matrix products  29.8 us (7%)
  local copies, waits for them, and re-layouts  16.5 us (4%)
  between operations  14.9 us (3%)
  loops' own time  11 us (3%)
  waiting for transfers between devices  10.4 us (2%)
  other arithmetic  8.58 us (2%)
    psum x2, blocking collectives, shards(): summed = lax.psum(partial_spend, 'imp')  146 us
    squeeze x2, blocking collectives, shards(): whole_prices = lax.all_gather(prices, 'imp', axis=1, tiled=True)[0]  136 us
    dot_general x16, matrix products, scored(): lax.dot_general(impressions, panel_rows, (((1,), (1,)), ((), ())), prefer...  29.8 us
    pmax x2, blocking collectives, shards(): merged_top = lax.pmax(row_top, 'cre')  29.1 us
    psum x2, blocking collectives, shards(): row_total = lax.psum(row_total * jnp.exp(row_top - merged_top), 'cre')  25.2 us
    another operation x4, loops' own time, sweep(): lax.scan(inner, running, jnp.arange(col_count // sub_width, dtype=jnp.int...  11 us
    all_gather x1, waiting for transfers between devices, shards(): lax.all_gather(panels, 'imp', axis=1, tiled=True)[0]  9.76 us
    dynamic_slice x16, local copies, waits for them, and re-layouts, sweep(): lax.scan(inner, running, jnp.arange(col_count // sub_width, dtype=jnp.int...  9.67 us
  transfers between devices with their start and end apart: 1, of which 1 were waited for; matrix products, arithmetic and copies ran while one was open for 1% of the time, Pallas kernels for 0%

commit v1 on v0

--- a/solution.py
+++ b/solution.py
@@ -10,6 +10,11 @@
 NEG_FILL = -1e30
 TAU_INV = 4.0
 STEP_RATE = 0.5
+
+
+def all_by_exchange(array, name, d):
+    sent = jnp.stack([array] * lax.axis_size(name))
+    return jnp.concatenate(lax.all_to_all(sent, name, 0, 0), axis=d)
 
 
 def block_table(block_lists, block_counts, local_blocks, cre_index):
@@ -90,11 +95,7 @@
             return lax.dynamic_update_slice_in_dim(current, col_spend, first_col, 0)
 
         partial_spend = sweep(
-            lax.all_gather(panels, "imp", axis=1, tiled=True)[0],
-            whole_prices,
-            mask_full,
-            empty_spend,
-            spend_step,
+            all_by_exchange(panels, "imp", 1)[0], whole_prices, mask_full, empty_spend, spend_step
         )
         summed = lax.psum(partial_spend, "imp")
         spend_owned = lax.dynamic_slice_in_dim(summed, owned_start, owned_rows, 0)

time: 429 us -> 445 us (1.037)
  blocking collectives: 337 us -> 350 us
  starting transfers between devices: 0.04 us -> 12.8 us
  waiting for transfers between devices: 10.4 us -> 0.7 us
    squeeze x2, blocking collectives: 136 us -> 150 us  [shards(): whole_prices = lax.all_gather(prices, 'imp', axis=1, tiled=True)[0]]
    all_to_all x0 -> x1, starting transfers between devices: none -> 12.8 us  [all_by_exchange(): return jnp.concatenate(lax.all_to_all(sent, name, 0, 0), axis=d)]
    all_gather x1, waiting for transfers between devices: 9.76 us -> 0.02 us  [shards(): lax.all_gather(panels, 'imp', axis=1, tiled=True)[0]]
  transfers between devices with their start and end apart: 1 -> 2, of which waited for: 1 -> 0; matrix products, arithmetic and copies ran while one was open for 1% -> 4% of each run, Pallas kernels for 0% -> 0%
where the time goes in v1:
time: 445 us; the launch traced here: 443 us
  blocking collectives  350 us (79%)
  matrix products  30.5 us (7%)
  local copies, waits for them, and re-layouts  16.2 us (4%)
  between operations  15 us (3%)
  starting transfers between devices  12.8 us (3%)
  loops' own time  10.8 us (2%)
  other arithmetic  7.22 us (2%)
    squeeze x2, blocking collectives, shards(): whole_prices = lax.all_gather(prices, 'imp', axis=1, tiled=True)[0]  150 us
    psum x2, blocking collectives, shards(): summed = lax.psum(partial_spend, 'imp')  146 us
    dot_general x16, matrix products, scored(): lax.dot_general(impressions, panel_rows, (((1,), (1,)), ((), ())), prefer...  30.5 us
    pmax x2, blocking collectives, shards(): merged_top = lax.pmax(row_top, 'cre')  29.3 us
    psum x2, blocking collectives, shards(): row_total = lax.psum(row_total * jnp.exp(row_top - merged_top), 'cre')  25.2 us
    all_to_all x1, starting transfers between devices, all_by_exchange(): return jnp.concatenate(lax.all_to_all(sent, name, 0, 0), axis=d)  12.8 us
    another operation x4, loops' own time, sweep(): lax.scan(inner, running, jnp.arange(col_count // sub_width, dtype=jnp.int...  10.8 us
    dynamic_slice x16, local copies, waits for them, and re-layouts, sweep(): lax.scan(inner, running, jnp.arange(col_count // sub_width, dtype=jnp.int...  9.39 us
  transfers between devices with their start and end apart: 2, of which 0 were waited for; matrix products, arithmetic and copies ran while one was open for 4% of the time, Pallas kernels for 0%

profile of v1, /device:TPU:1, one launch (start us, length us, event | category | flops | bytes accessed | tf_op | source)
XLA Modules:
  0.0 443.0 jit_solution(8327474467549978428)
XLA Ops:
  7.3 0.7 all-gather.2.cloned.1.call-update
  7.9 1.9 stack.2
  9.9 12.8 %all-to-all-start = ((bf16[32,1,64,256]{3,2,1,0:T(8,128)(2,1)}), bf16[32,1,64,256]{3,2,1,0:T(8,128)(2,1)S(1)}, u32[]{:S(2)}, u32[]{:S(2)}) async-start(bf16[32,1,64,256]{3,2,1,0:T(8,128)(2,1)} %stack.2), calls=%async_computation | async-start | bytes 2097152 | tf_op jit(solution)/shard_map/all_to_all | solution.py:17
  24.5 83.6 %all-reduce = f32[2048]{0:T(1024)S(1)} all-reduce(f32[2048]{0:T(1024)S(1)} %bitcast_dynamic-update-slice_fusion.1), channel_id=1, replica_groups=mesh['imp'=32,'cre'=8] {'imp'}, use_global_device_ids=true, to_apply=%add | all-reduce | flops 2048 | bytes 16384 | tf_op jit(solution)/shard_map/squeeze | solution.py:78
  108.7 15.4 %while.48 = (s32[]{:T(128)}, f32[1024]{0:T(1024)S(1)}, f32[1024]{0:T(1024)S(1)}, s32[4]{0:T(128)S(1)}, pred[1024,2048]{0,1:T(32,128)(4,1)S(1)}, /*index=5*/bf16[...) while((s32[]{:T(128)}, f32[1024]{0:T(1024)S(1)}, ...), condition=%wide.region_4.5_spmd.clone, body=%wide.region_1.4_spmd.clone.sunk | while | flops 273684480 | bytes 6075585 | solution.py:48
  108.7 0.6 dynamic_slice.118
  110.0 1.7 fusion.49
  111.7 0.8 select_reduce_fusion.4
  112.5 0.6 dynamic_slice.118
  113.8 1.7 fusion.49
  115.6 0.8 select_reduce_fusion.4
  116.4 0.6 dynamic_slice.118
  117.7 1.7 fusion.49
  119.5 0.8 select_reduce_fusion.4
  120.3 0.6 dynamic_slice.118
  121.6 1.7 fusion.49
  123.3 0.8 select_reduce_fusion.4
  124.1 15.1 %pmax.14 = f32[1024]{0:T(1024)S(1)} all-reduce(f32[1024]{0:T(1024)S(1)} %get-tuple-element.183), channel_id=1, replica_groups=mesh['imp'=32,'cre'=8] {'cre'}, use_global_device_ids=true, to_apply=%region_5.6 | all-reduce | flops 1024 | bytes 8192 | tf_op jit(solution)/shard_map/pmax | solution.py:86
  139.2 12.5 %psum.28 = f32[1024]{0:T(1024)S(1)} all-reduce(f32[1024]{0:T(1024)S(1)} %exponential_multiply_fusion.1), channel_id=1, replica_groups=mesh['imp'=32,'cre'=8] {'cre'}, use_global_device_ids=true, to_apply=%region_6.7 | all-reduce | flops 1024 | bytes 8192 | tf_op jit(solution)/shard_map/psum | solution.py:87
  151.7 14.6 %while.46 = (s32[]{:T(128)}, f32[2048]{0:T(1024)S(1)}, f32[1024]{0:T(1024)S(1)}, s32[4]{0:T(128)S(1)}, pred[1024,2048]{0,1:T(32,128)(4,1)S(1)}, /*index=5*/bf16[...) while((s32[]{:T(128)}, f32[2048]{0:T(1024)S(1)}, ...), condition=%wide.region_9.10_spmd, body=%wide.region_7.9_spmd.sunk | while | flops 272104960 | bytes 1332415 | solution.py:48
  151.7 0.6 dynamic_slice.109
  153.0 2.1 fusion.44
  156.7 2.1 fusion.44
  160.4 2.1 fusion.44
  164.0 2.1 fusion.44
  166.3 72.7 %psum.29 = f32[2048]{0:T(1024)S(1)} all-reduce(f32[2048]{0:T(1024)S(1)} %get-tuple-element.185), channel_id=1, replica_groups=mesh['imp'=32,'cre'=8] {'imp'}, use_global_device_ids=true, to_apply=%region_10.11 | all-reduce | flops 2048 | bytes 16384 | tf_op jit(solution)/shard_map/psum | solution.py:100
  239.3 66.0 %all-reduce.1 = f32[2048]{0:T(1024)S(1)} all-reduce(f32[2048]{0:T(1024)S(1)} %get-tuple-element.317), channel_id=1, replica_groups=mesh['imp'=32,'cre'=8] {'imp'}, use_global_device_ids=true, to_apply=%add.1 | all-reduce | flops 2048 | bytes 16384 | tf_op jit(solution)/shard_map/squeeze | solution.py:78
  305.4 15.5 %while.49 = (s32[]{:T(128)}, f32[1024]{0:T(1024)S(1)}, f32[1024]{0:T(1024)S(1)}, s32[4]{0:T(128)S(1)}, pred[1024,2048]{0,1:T(32,128)(4,1)S(1)}, /*index=5*/bf16[...) while((s32[]{:T(128)}, f32[1024]{0:T(1024)S(1)}, ...), condition=%wide.region_14.15_spmd.clone, body=%wide.region_11.14_spmd.clone.sunk | while | flops 273684480 | bytes 6075585 | solution.py:48
  305.4 0.6 dynamic_slice.123
  306.7 1.7 fusion.52
  308.4 0.8 select_reduce_fusion.5
  309.2 0.6 dynamic_slice.123
  310.6 1.7 fusion.52
  312.3 0.8 select_reduce_fusion.5
  314.5 1.7 fusion.52
  316.2 0.8 select_reduce_fusion.5
  317.0 0.6 dynamic_slice.123
  318.3 1.7 fusion.52
  320.1 0.8 select_reduce_fusion.5
  320.9 14.2 %pmax.15 = f32[1024]{0:T(1024)S(1)} all-reduce(f32[1024]{0:T(1024)S(1)} %get-tuple-element.186), channel_id=1, replica_groups=mesh['imp'=32,'cre'=8] {'cre'}, use_global_device_ids=true, to_apply=%region_15.16 | all-reduce | flops 1024 | bytes 8192 | tf_op jit(solution)/shard_map/pmax | solution.py:86
  335.1 12.7 %psum.30 = f32[1024]{0:T(1024)S(1)} all-reduce(f32[1024]{0:T(1024)S(1)} %exponential_multiply_fusion), channel_id=1, replica_groups=mesh['imp'=32,'cre'=8] {'cre'}, use_global_device_ids=true, to_apply=%region_16.17 | all-reduce | flops 1024 | bytes 8192 | tf_op jit(solution)/shard_map/psum | solution.py:87
  347.9 14.6 %while.47 = (s32[]{:T(128)}, f32[2048]{0:T(1024)S(1)}, f32[1024]{0:T(1024)S(1)}, s32[4]{0:T(128)S(1)}, pred[1024,2048]{0,1:T(32,128)(4,1)S(1)}, /*index=5*/bf16[...) while((s32[]{:T(128)}, f32[2048]{0:T(1024)S(1)}, ...), condition=%wide.region_19.20_spmd, body=%wide.region_17.19_spmd.sunk | while | flops 272104960 | bytes 1332415 | solution.py:48
  349.2 2.1 fusion.47
  352.9 2.1 fusion.47
  356.5 2.1 fusion.47
  360.2 2.1 fusion.47
  362.5 73.0 %psum.31 = f32[2048]{0:T(1024)S(1)} all-reduce(f32[2048]{0:T(1024)S(1)} %get-tuple-element.188), channel_id=1, replica_groups=mesh['imp'=32,'cre'=8] {'imp'}, use_global_device_ids=true, to_apply=%region_20.21 | all-reduce | flops 2048 | bytes 16384 | tf_op jit(solution)/shard_map/psum | solution.py:100
  435.5 0.6 multiply_add_fusion
  (83 shorter events, 10.1 us)
Async XLA Ops:
  7.2 15.9 %copy-start.6 = (u32[256]{0:T(256)S(1)}, u32[256]{0:T(256)}, u32[]{:S(2)}) copy-start(u32[256]{0:T(256)} %constant.107) | copy-start | bytes 3076
  7.2 15.5 %copy-start.5 = (s32[8]{0:T(128)S(1)}, s32[8]{0:T(128)}, u32[]{:S(2)}) copy-start(s32[8]{0:T(128)} %param.18) | copy-start | bytes 100
  7.2 15.6 %copy-start.1 = (s32[8,16]{1,0:T(8,128)S(1)}, s32[8,16]{1,0:T(8,128)}, u32[]{:S(2)}) copy-start(s32[8,16]{1,0:T(8,128)} %param.17) | copy-start | bytes 1540
  7.2 17.2 %copy-start.3 = (f32[1,64]{1,0:T(1,128)S(1)}, f32[1,64]{1,0:T(1,128)}, u32[]{:S(2)}) copy-start(f32[1,64]{1,0:T(1,128)} %param.21) | copy-start | bytes 772
  7.2 100.9 %all-gather.2.cloned.1.call-start = ((), (), s32[]{:S(2)}) async-start(), calls=%async_computation.1 | async-start | bytes 1081344 | tf_op jit(solution)/shard_map/all_gather | solution.py:80
  9.9 141.8 %all-to-all-start = ((bf16[32,1,64,256]{3,2,1,0:T(8,128)(2,1)}), bf16[32,1,64,256]{3,2,1,0:T(8,128)(2,1)S(1)}, u32[]{:S(2)}, u32[]{:S(2)}) async-start(bf16[32,1,64,256]{3,2,1,0:T(8,128)(2,1)} %stack.2), calls=%async_computation | async-start | bytes 2097152 | tf_op jit(solution)/shard_map/all_to_all | solution.py:17
  108.7 43.0 %copy-start.4 = (f32[1024]{0:T(1024)S(1)}, f32[1024]{0:T(1024)}, u32[]{:S(2)}) copy-start(f32[1024]{0:T(1024)} %param.19) | copy-start | bytes 12292
  151.7 87.4 %copy-start.2 = (f32[1,64]{1,0:T(1,128)S(1)}, f32[1,64]{1,0:T(1,128)}, u32[]{:S(2)}) copy-start(f32[1,64]{1,0:T(1,128)} %param.20) | copy-start | bytes 772
  362.5 73.6 %copy-start = (f32[1024]{0:T(1024)}, f32[1024]{0:T(1024)S(1)}, u32[]{:S(2)}) copy-start(f32[1024]{0:T(1024)S(1)} %get-tuple-element.707) | copy-start | bytes 12292
Sparse Core Ops, SparseCore 0:
  10.8 84.2 all-gather.1
